TPU v7x, 256 devices: a whole 4x4x8 slice. The times are simulated.
256 devices in a mesh: grp: 16 (over z, core), head: 16 (over y, x).
Axes of the slice: x: 4, y: 4, z: 8, core: 2. Of those that a mesh axis runs over, the one named last changes fastest.
Arguments:
- query_rows: bfloat16 [256, 128, 2048], P(('grp', 'head')), may hold values from -6 to 6
- key_rows: bfloat16 [256, 128, 2048], P(('grp', 'head')), may hold values from -6 to 6
- value_rows: bfloat16 [256, 128, 2048], P(('grp', 'head')), may hold values from -6 to 6
- log_decay: bfloat16 [256, 128, 2048], P(('grp', 'head')), may hold values from -1.5 to 0, as said below
- beta_logit: bfloat16 [256, 128, 16], P(('grp', 'head')), may hold values from -6 to 6
- out_grad: bfloat16 [256, 128, 2048], P(('grp', 'head')), may hold values from -6 to 6
- fork_state: float32 [8, 16, 128, 128], P(None, 'head'), may hold values from -6 to 6
- branch_prompt: int32 [256], replicated, may hold values from 0 to 7, as said below
- valid_len: int32 [256], replicated, may hold values from 32 to 128, as said below
Outputs:
- grad_query: bfloat16 [256, 128, 2048], P(('grp', 'head'))
- grad_key: bfloat16 [256, 128, 2048], P(('grp', 'head'))
- grad_value: bfloat16 [256, 128, 2048], P(('grp', 'head'))
- grad_decay: bfloat16 [256, 128, 2048], P(('grp', 'head'))
- grad_beta: bfloat16 [256, 128, 16], P(('grp', 'head'))
- grad_fork: float32 [8, 16, 128, 128], P(None, 'head')
Inputs may be any that keep to these rules, and one draw needn't show every extreme that they name: `log_decay`: never positive; a few tokens of each branch lose a large share of every channel at once. `branch_prompt`: every prompt has at least one branch. A branch counts its first valid_len tokens; some branch uses all 128.
All inputs are finite; a program needn't handle non-finite values.
Results may differ from a plain program's by a relative error of at most 0.0015.
Values may be sent and summed in bfloat16 or wider, within the bound.
A program may use at most 64 MiB of HBM per device.

v0:
```python
from functools import partial
import jax
import jax.numpy as jnp
from jax import lax
from jax.sharding import PartitionSpec as P


def decay_forward(query_in, key_in, value_in, decay_in, beta_in, state_in, keep_mask, block_len):
    head_dim = query_in.shape[-1]
    upper_limit = lax.Precision.HIGHEST
    unit_query = (
        query_in
        * lax.rsqrt(jnp.sum(query_in * query_in, axis=-1, keepdims=True) + 1e-06)
        * head_dim ** (-0.5)
    )
    unit_key = key_in * lax.rsqrt(jnp.sum(key_in * key_in, axis=-1, keepdims=True) + 1e-06)
    beta_value = jax.nn.sigmoid(beta_in) * keep_mask[None, :]
    decay_value = decay_in * keep_mask[None, :, None]
    token_positions = jnp.arange(block_len, dtype=jnp.int32)
    lower_strict = (token_positions[:, None] > token_positions[None, :]).astype(jnp.float32)
    lower_closed = (token_positions[:, None] >= token_positions[None, :]).astype(jnp.float32)
    identity_block = jnp.eye(block_len, dtype=jnp.float32)
    cum_decay = jnp.cumsum(decay_value, axis=1)
    growth = jnp.exp(cum_decay)
    shrink = jnp.exp(-cum_decay)
    key_forward_rows = unit_key * growth
    key_earlier_rows = unit_key * shrink
    query_forward_rows = unit_query * growth
    coupling = (
        jnp.einsum("htk,hsk->hts", key_forward_rows, key_earlier_rows, precision=upper_limit)
        * beta_value[:, :, None]
        * lower_strict
    )
    attend_scores = (
        jnp.einsum("htk,hsk->hts", query_forward_rows, key_earlier_rows, precision=upper_limit)
        * lower_closed
    )
    target_output = beta_value[:, :, None] * (
        value_in - jnp.einsum("led,ldf->lef", key_forward_rows, state_in, precision=upper_limit)
    )
    state_update = jax.scipy.linalg.solve_triangular(
        identity_block + coupling, target_output, lower=True, unit_diagonal=True
    )
    output_block_rows = jnp.einsum(
        "led,ldf->lef", query_forward_rows, state_in, precision=upper_limit
    ) + jnp.einsum("ifj,ijo->ifo", attend_scores, state_update, precision=upper_limit)
    outputs = [output_block_rows]
    return jnp.concatenate(outputs, axis=1)


def branch_backward(
    query_rows, key_rows, value_rows, log_decay, out_grad, beta_logit, states, valid_rows, block_len
):
    count, window_len, row_width = query_rows.shape
    heads_here = states.shape[1]
    head_dim = states.shape[-1]

    def split_heads(array_in):
        return (
            array_in.astype(jnp.float32)
            .reshape(count, window_len, heads_here, head_dim)
            .transpose(0, 2, 1, 3)
        )

    def join_heads(array_in):
        return (
            array_in.transpose(0, 2, 1, 3)
            .reshape(count, window_len, row_width)
            .astype(jnp.bfloat16)
        )

    keep_mask = (jnp.arange(window_len, dtype=jnp.int32)[None, :] < valid_rows[:, None]).astype(
        jnp.float32
    )
    beta_in = beta_logit.astype(jnp.float32).transpose(0, 2, 1)
    mapped = jax.vmap(partial(decay_forward, block_len=block_len))

    def forward_all(query_in, key_in, value_in, decay_in, beta_all, state_all):
        return mapped(query_in, key_in, value_in, decay_in, beta_all, state_all, keep_mask)

    outputs, pullback = jax.vjp(
        forward_all,
        split_heads(query_rows),
        split_heads(key_rows),
        split_heads(value_rows),
        split_heads(log_decay),
        beta_in,
        states,
    )
    cotangent = split_heads(out_grad) * keep_mask[:, None, :, None]
    grad_q, grad_k, grad_v, grad_g, grad_b, grad_s = pullback(cotangent)
    gradients = (
        join_heads(grad_q),
        join_heads(grad_k),
        join_heads(grad_v),
        join_heads(grad_g),
        grad_b.transpose(0, 2, 1).astype(jnp.bfloat16),
    )
    return (gradients, grad_s)


def per_device(
    query_rows,
    key_rows,
    value_rows,
    log_decay,
    beta_logit,
    out_grad,
    fork_state,
    branch_prompt,
    valid_len,
):
    upper_limit = lax.Precision.HIGHEST
    local_count = query_rows.shape[0]
    head_count = lax.axis_size("head")
    group_size = local_count * head_count
    group_first = lax.axis_index("grp") * group_size
    prompt_count = fork_state.shape[0]
    prompt_ids = jnp.arange(prompt_count, dtype=jnp.int32)
    window_len = query_rows.shape[1]
    group_prompt = lax.dynamic_slice_in_dim(branch_prompt, group_first, group_size)
    group_onehot = (group_prompt[:, None] == prompt_ids[None, :]).astype(jnp.float32)
    group_states = jnp.einsum("bp,phij->bhij", group_onehot, fork_state, precision=upper_limit)
    arrived = (
        lax.all_to_all(query_rows, "head", split_axis=2, concat_axis=0, tiled=True),
        lax.all_to_all(key_rows, "head", split_axis=2, concat_axis=0, tiled=True),
        lax.all_to_all(value_rows, "head", split_axis=2, concat_axis=0, tiled=True),
        lax.all_to_all(log_decay, "head", split_axis=2, concat_axis=0, tiled=True),
        lax.all_to_all(out_grad, "head", split_axis=2, concat_axis=0, tiled=True),
        lax.all_to_all(beta_logit, "head", split_axis=2, concat_axis=0, tiled=True),
    )
    group_len = lax.dynamic_slice_in_dim(valid_len, group_first, group_size)
    gradients, state_grad = branch_backward(
        arrived[0],
        arrived[1],
        arrived[2],
        arrived[3],
        arrived[4],
        arrived[5],
        group_states,
        group_len,
        window_len,
    )
    prompt_grad = jnp.einsum("bp,bhij->phij", group_onehot, state_grad, precision=upper_limit)
    results = (
        lax.all_to_all(gradients[0], "head", split_axis=0, concat_axis=2, tiled=True),
        lax.all_to_all(gradients[1], "head", split_axis=0, concat_axis=2, tiled=True),
        lax.all_to_all(gradients[2], "head", split_axis=0, concat_axis=2, tiled=True),
        lax.all_to_all(gradients[3], "head", split_axis=0, concat_axis=2, tiled=True),
        lax.all_to_all(gradients[4], "head", split_axis=0, concat_axis=2, tiled=True),
    )
    grad_fork = lax.psum(prompt_grad, "grp")
    return (results[0], results[1], results[2], results[3], results[4], grad_fork)


def solution(mesh):
    return jax.shard_map(
        per_device,
        mesh=mesh,
        in_specs=(
            P(("grp", "head"), None, None),
            P(("grp", "head"), None, None),
            P(("grp", "head"), None, None),
            P(("grp", "head"), None, None),
            P(("grp", "head"), None, None),
            P(("grp", "head"), None, None),
            P(None, "head", None, None),
            P(),
            P(),
        ),
        out_specs=(
            P(("grp", "head"), None, None),
            P(("grp", "head"), None, None),
            P(("grp", "head"), None, None),
            P(("grp", "head"), None, None),
            P(("grp", "head"), None, None),
            P(None, "head", None, None),
        ),
        check_vma=False,
    )
```

profile of v0, /device:TPU:1, one launch (start us, length us, event | category | flops | bytes accessed | tf_op | source)
XLA Modules:
  0.0 567.9 jit_solution(9979392489376102869)
XLA Ops:
  8.5 7.6 %all-to-all-start.3 = ((bf16[1,128,16]{1,0,2:T(2,128)(2,1)}), bf16[1,128,16]{1,0,2:T(2,128)(2,1)S(1)}, u32[]{:S(2)}, u32[]{:S(2)}) async-start(bf16[1,128,16]{1,0,2:T(2,128)(2,1)} %copy.205), calls=%async_computation.3 | async-start | bytes 16384 | tf_op jit(solution)/shard_map/all_to_all | solution.py:130
  19.8 11.5 %reduce.13 = bf16[2048,128]{1,0:T(8,128)(2,1)S(1)} reduce(bf16[2048,1,128]{2,1,0:T(2,128)(2,1)S(1)} %bitcast.201, bf16[]{:T(256)} %broadcast.315), dimensions={1}, to_apply=%bitcast.156.reduce_sub_computation | reduce | bytes 1048578
  32.3 7.0 %all-to-all-start.5 = ((bf16[16,2,8192]{2,1,0:T(2,128)(2,1)}), bf16[16,2,8192]{2,1,0:T(2,128)(2,1)S(1)}, u32[]{:S(2)}, u32[]{:S(2)}) async-start(bf16[16,2,8192]{2,1,0:T(2,128)(2,1)} %reshape.506), calls=%async_computation.5 | async-start | bytes 1048576 | tf_op jit(solution)/shard_map/all_to_all | solution.py:125
  40.0 11.5 %reduce.10 = bf16[2048,128]{1,0:T(8,128)(2,1)S(1)} reduce(bf16[2048,1,128]{2,1,0:T(2,128)(2,1)S(1)} %bitcast.205, bf16[]{:T(256)} %broadcast.315), dimensions={1}, to_apply=%bitcast.158.reduce_sub_computation | reduce | bytes 1048578
  53.4 11.5 %reduce.11 = bf16[2048,128]{1,0:T(8,128)(2,1)S(1)} reduce(bf16[2048,1,128]{2,1,0:T(2,128)(2,1)S(1)} %bitcast.206, bf16[]{:T(256)} %broadcast.315), dimensions={1}, to_apply=%bitcast.162.reduce_sub_computation | reduce | bytes 1048578
  66.7 11.7 %reduce.12 = bf16[2048,128]{1,0:T(8,128)(2,1)S(1)} reduce(bf16[2048,1,128]{2,1,0:T(2,128)(2,1)S(1)} %bitcast.207, bf16[]{:T(256)} %broadcast.315), dimensions={1}, to_apply=%bitcast.160.reduce_sub_computation | reduce | bytes 1048578
  80.3 11.5 %reduce.14 = bf16[2048,128]{1,0:T(8,128)(2,1)S(1)} reduce(bf16[2048,1,128]{2,1,0:T(2,128)(2,1)S(1)} %bitcast.202, bf16[]{:T(256)} %broadcast.315), dimensions={1}, to_apply=%bitcast.164.reduce_sub_computation | reduce | bytes 1048578
  94.7 6.7 %all-to-all-start.1 = ((bf16[16,2,8192]{2,1,0:T(2,128)(2,1)}), bf16[16,2,8192]{2,1,0:T(2,128)(2,1)S(1)}, u32[]{:S(2)}, u32[]{:S(2)}) async-start(bf16[16,2,8192]{2,1,0:T(2,128)(2,1)} %reshape.508), calls=%async_computation.1 | async-start | bytes 1048576 | tf_op jit(solution)/shard_map/all_to_all | solution.py:126
  103.1 7.9 %all-to-all-done.1 = bf16[16,2,8192]{2,1,0:T(2,128)(2,1)S(1)} async-done(((bf16[16,2,8192]{2,1,0:T(2,128)(2,1)}), bf16[16,2,8192]{2,1,0:T(2,128)(2,1)S(1)}, u32[]{:S(2)}, u32[]{:S(2)}) %all-to-all-start.1) | async-done | bytes 524320 | tf_op jit(solution)/shard_map/all_to_all | solution.py:126
  111.0 4.6 all-to-all-start.2
  117.6 7.1 %all-to-all-done.2 = bf16[16,2,8192]{2,1,0:T(2,128)(2,1)} async-done(((bf16[16,2,8192]{2,1,0:T(2,128)(2,1)}), bf16[16,2,8192]{2,1,0:T(2,128)(2,1)}, u32[]{:S(2)}, u32[]{:S(2)}) %all-to-all-start.2) | async-done | bytes 524320 | tf_op jit(solution)/shard_map/all_to_all | solution.py:128
  124.7 4.2 all-to-all-start
  143.5 157.8 %custom-call.7 = f32[16,1,128,128]{2,3,1,0:T(8,128)} custom-call(f32[16,1,128,128]{3,2,1,0:T(8,128)S(1)} %add_bitcast_fusion), custom_call_target="InvertDiagBlocksLowerTriangular" | custom-call | tf_op jit(solution)/shard_map/jvp(vmap(jit(_solve_triangular)))/triangular_solve | solution.py:41
  301.3 6.6 %all-to-all-start.4 = ((bf16[16,2,8192]{2,1,0:T(2,128)(2,1)}), bf16[16,2,8192]{2,1,0:T(2,128)(2,1)}, u32[]{:S(2)}, u32[]{:S(2)}) async-start(bf16[16,2,8192]{2,1,0:T(2,128)(2,1)} %reshape.514), calls=%async_computation.4 | async-start | bytes 1048576 | tf_op jit(solution)/shard_map/all_to_all | solution.py:127
  348.8 6.4 %all-to-all-start.10 = ((bf16[16,128,1]{1,2,0:T(2,128)(2,1)}), bf16[16,128,1]{1,2,0:T(2,128)(2,1)S(1)}, u32[]{:S(2)}, u32[]{:S(2)}) async-start(bf16[16,128,1]{1,2,0:T(2,128)(2,1)} %copy.235), calls=%async_computation.10 | async-start | bytes 16384 | tf_op jit(solution)/shard_map/all_to_all | solution.py:150
  355.3 4.2 fusion.31
  365.0 4.3 multiply_reduce_fusion.2
  376.4 6.7 %all-to-all-start.9 = ((bf16[16,128,128]{2,1,0:T(8,128)(2,1)}), bf16[16,128,128]{2,1,0:T(8,128)(2,1)}, u32[]{:S(2)}, u32[]{:S(2)}) async-start(bf16[16,128,128]{2,1,0:T(8,128)(2,1)} %copy.231), calls=%async_computation.9 | async-start | bytes 1048576 | tf_op jit(solution)/shard_map/all_to_all | solution.py:149
  387.1 5.0 all-to-all-done.9
  392.2 13.4 %all_to_all.144 = bf16[16,128,128]{1,2,0:T(8,128)(2,1)} all-to-all(bf16[16,128,128]{1,2,0:T(8,128)(2,1)} %get-tuple-element.45), channel_id=1, replica_groups=mesh['grp'=16,'head'=16] {'head'}, dimensions={0} | all-to-all | bytes 1048576 | tf_op jit(solution)/shard_map/all_to_all | solution.py:146
  405.5 4.5 all-to-all-start.7
  413.3 5.7 %all-to-all-done.7 = bf16[16,128,128]{1,2,0:T(8,128)(2,1)} async-done(((bf16[16,128,128]{1,2,0:T(8,128)(2,1)}), bf16[16,128,128]{1,2,0:T(8,128)(2,1)}, u32[]{:S(2)}, u32[]{:S(2)}) %all-to-all-start.7) | async-done | bytes 524320 | tf_op jit(solution)/shard_map/all_to_all | solution.py:147
  419.0 4.2 all-to-all-start.8
  429.1 121.8 %all-reduce.2.cloned.1.call-done = f32[8,1,128,128]{3,0,2,1:T(8,128)} async-done(((f32[8,1,128,128]{3,0,2,1:T(8,128)}), f32[8,1,128,128]{3,0,2,1:T(8,128)}) %all-reduce.2.cloned.1.call-update) | async-done | bytes 524304 | tf_op jit(solution)/shard_map/psum | solution.py:152
  (144 shorter events, 109.0 us)
Async XLA Ops:
  7.2 85.7 %copy-start = (f32[8,1,128,128]{3,2,1,0:T(8,128)S(1)}, f32[8,1,128,128]{3,2,1,0:T(8,128)}, u32[]{:S(2)}) copy-start(f32[8,1,128,128]{3,2,1,0:T(8,128)} %param.17) | copy-start | bytes 1572868
  8.5 23.7 %all-to-all-start.3 = ((bf16[1,128,16]{1,0,2:T(2,128)(2,1)}), bf16[1,128,16]{1,0,2:T(2,128)(2,1)S(1)}, u32[]{:S(2)}, u32[]{:S(2)}) async-start(bf16[1,128,16]{1,0,2:T(2,128)(2,1)} %copy.205), calls=%async_computation.3 | async-start | bytes 16384 | tf_op jit(solution)/shard_map/all_to_all | solution.py:130
  32.2 7.0 %copy-start.24 = (bf16[1,128,2048]{2,1,0:T(8,128)(2,1)S(1)}, bf16[1,128,2048]{2,1,0:T(8,128)(2,1)}, u32[]{:S(2)}) copy-start(bf16[1,128,2048]{2,1,0:T(8,128)(2,1)} %param.12) | copy-start | bytes 1572868
  32.3 62.4 %all-to-all-start.5 = ((bf16[16,2,8192]{2,1,0:T(2,128)(2,1)}), bf16[16,2,8192]{2,1,0:T(2,128)(2,1)S(1)}, u32[]{:S(2)}, u32[]{:S(2)}) async-start(bf16[16,2,8192]{2,1,0:T(2,128)(2,1)} %reshape.506), calls=%async_computation.5 | async-start | bytes 1048576 | tf_op jit(solution)/shard_map/all_to_all | solution.py:125
  94.7 16.4 %all-to-all-start.1 = ((bf16[16,2,8192]{2,1,0:T(2,128)(2,1)}), bf16[16,2,8192]{2,1,0:T(2,128)(2,1)S(1)}, u32[]{:S(2)}, u32[]{:S(2)}) async-start(bf16[16,2,8192]{2,1,0:T(2,128)(2,1)} %reshape.508), calls=%async_computation.1 | async-start | bytes 1048576 | tf_op jit(solution)/shard_map/all_to_all | solution.py:126
  111.0 13.7 %all-to-all-start.2 = ((bf16[16,2,8192]{2,1,0:T(2,128)(2,1)}), bf16[16,2,8192]{2,1,0:T(2,128)(2,1)}, u32[]{:S(2)}, u32[]{:S(2)}) async-start(bf16[16,2,8192]{2,1,0:T(2,128)(2,1)} %reshape.512), calls=%async_computation.2 | async-start | bytes 1048576 | tf_op jit(solution)/shard_map/all_to_all | solution.py:128
  124.7 176.6 %all-to-all-start = ((bf16[16,2,8192]{2,1,0:T(2,128)(2,1)}), bf16[16,2,8192]{2,1,0:T(2,128)(2,1)}, u32[]{:S(2)}, u32[]{:S(2)}) async-start(bf16[16,2,8192]{2,1,0:T(2,128)(2,1)} %reshape.510), calls=%async_computation | async-start | bytes 1048576 | tf_op jit(solution)/shard_map/all_to_all | solution.py:129
  139.2 2.9 copy-start.4
  301.3 15.7 %all-to-all-start.4 = ((bf16[16,2,8192]{2,1,0:T(2,128)(2,1)}), bf16[16,2,8192]{2,1,0:T(2,128)(2,1)}, u32[]{:S(2)}, u32[]{:S(2)}) async-start(bf16[16,2,8192]{2,1,0:T(2,128)(2,1)} %reshape.514), calls=%async_computation.4 | async-start | bytes 1048576 | tf_op jit(solution)/shard_map/all_to_all | solution.py:127
  330.2 2.2 copy-start.19
  342.4 2.4 copy-start.17
  348.8 27.6 %all-to-all-start.10 = ((bf16[16,128,1]{1,2,0:T(2,128)(2,1)}), bf16[16,128,1]{1,2,0:T(2,128)(2,1)S(1)}, u32[]{:S(2)}, u32[]{:S(2)}) async-start(bf16[16,128,1]{1,2,0:T(2,128)(2,1)} %copy.235), calls=%async_computation.10 | async-start | bytes 16384 | tf_op jit(solution)/shard_map/all_to_all | solution.py:150
  355.2 4.2 copy-start.8
  355.2 4.2 copy-start.15
  361.0 2.3 copy-start.6
  361.0 2.3 copy-start.20
  364.7 4.5 copy-start.14
  376.4 15.8 %all-to-all-start.9 = ((bf16[16,128,128]{2,1,0:T(8,128)(2,1)}), bf16[16,128,128]{2,1,0:T(8,128)(2,1)}, u32[]{:S(2)}, u32[]{:S(2)}) async-start(bf16[16,128,128]{2,1,0:T(8,128)(2,1)} %copy.231), calls=%async_computation.9 | async-start | bytes 1048576 | tf_op jit(solution)/shard_map/all_to_all | solution.py:149
  392.2 17.9 %copy-start.9 = (f32[16,1,128,128]{2,3,0,1:T(8,128)S(1)}, f32[16,1,128,128]{2,3,0,1:T(8,128)}, u32[]{:S(2)}) copy-start(f32[16,1,128,128]{2,3,0,1:T(8,128)} %get-tuple-element.46) | copy-start | bytes 3145732
  405.5 13.5 %all-to-all-start.7 = ((bf16[16,128,128]{1,2,0:T(8,128)(2,1)}), bf16[16,128,128]{1,2,0:T(8,128)(2,1)}, u32[]{:S(2)}, u32[]{:S(2)}) async-start(bf16[16,128,128]{1,2,0:T(8,128)(2,1)} %get-tuple-element.44), calls=%async_computation.7 | async-start | bytes 1048576 | tf_op jit(solution)/shard_map/all_to_all | solution.py:147
  410.0 13.3 %copy-start.18 = (f32[16,128,128]{2,1,0:T(8,128)S(1)}, f32[16,128,128]{2,1,0:T(8,128)}, u32[]{:S(2)}) copy-start(f32[16,128,128]{2,1,0:T(8,128)} %get-tuple-element.50) | copy-start | bytes 3145732
  413.3 10.0 %copy-start.7 = (f32[16,1,128,128]{2,3,0,1:T(8,128)S(1)}, f32[16,1,128,128]{2,3,0,1:T(8,128)}, u32[]{:S(2)}) copy-start(f32[16,1,128,128]{2,3,0,1:T(8,128)} %copy-done.4) | copy-start | bytes 3145732
  419.0 139.2 %all-to-all-start.8 = ((bf16[16,128,128]{2,1,0:T(8,128)(2,1)}), bf16[16,128,128]{2,1,0:T(8,128)(2,1)}, u32[]{:S(2)}, u32[]{:S(2)}) async-start(bf16[16,128,128]{2,1,0:T(8,128)(2,1)} %get-tuple-element.43), calls=%async_computation.8 | async-start | bytes 1048576 | tf_op jit(solution)/shard_map/all_to_all | solution.py:148
  423.3 127.6 %all-reduce.2.cloned.1.call-start = ((), (), s32[]{:S(2)}) async-start(), calls=%async_computation.11 | async-start | bytes 1048576 | tf_op jit(solution)/shard_map/psum | solution.py:152
  (17 other events, 20.8 us)
Sparse Core Ops, SparseCore 0:
  428.6 122.2 all-reduce.1
where the time goes:
time: 575 us; the launch traced here: 568 us
  other arithmetic  234 us (41%)
  waiting for transfers between devices  148 us (26%)
  starting transfers between devices  58.7 us (10%)
  local copies, waits for them, and re-layouts  51.4 us (9%)
  matrix products  47.3 us (8%)
  between operations  15.1 us (3%)
  blocking collectives  13.4 us (2%)
    another operation x4, other arithmetic, decay_forward(): jax.scipy.linalg.solve_triangular(identity_block + coupling, target_outpu...  158 us
    psum x1, waiting for transfers between devices, per_device(): grad_fork = lax.psum(prompt_grad, 'grp')  122 us
    unnamed x5, other arithmetic  57.9 us
    unnamed x83, local copies, waits for them, and re-layouts  32.9 us
    all_to_all x1, blocking collectives, per_device(): lax.all_to_all(gradients[0], 'head', split_axis=0, concat_axis=2, tiled=T...  13.4 us
  transfers between devices with their start and end apart: 11, of which 6 were waited for; matrix products, arithmetic and copies ran while one was open for 52% of the time, Pallas kernels for 0%

commit v1 on v0

--- a/solution.py
+++ b/solution.py
@@ -149,7 +149,11 @@
         lax.all_to_all(gradients[3], "head", split_axis=0, concat_axis=2, tiled=True),
         lax.all_to_all(gradients[4], "head", split_axis=0, concat_axis=2, tiled=True),
     )
-    grad_fork = lax.psum(prompt_grad, "grp")
+    grad_fork = prompt_grad
+    for hop in (1, 2, 4, 8):
+        grad_fork = grad_fork + lax.ppermute(
+            grad_fork, "grp", [(dev, dev ^ hop) for dev in range(16)]
+        )
     return (results[0], results[1], results[2], results[3], results[4], grad_fork)
 
 

time: 575 us -> 477 us (0.83)
  waiting for transfers between devices: 148 us -> 49 us
  starting transfers between devices: 58.7 us -> 80.1 us
  between operations: 15.1 us -> 1.67 us
  blocking collectives: 13.4 us -> 0 us
  matrix products: 47.3 us -> 54.3 us
    psum x1 -> x0, waiting for transfers between devices: 122 us -> none  [per_device(): grad_fork = lax.psum(prompt_grad, 'grp')]
    ppermute x0 -> x4, waiting for transfers between devices: none -> 21.1 us  [per_device(): lax.ppermute(grad_fork, 'grp', [(dev, dev ^ hop) for dev in range(16)])]
    ppermute x0 -> x4, starting transfers between devices: none -> 15.9 us  [per_device(): lax.ppermute(grad_fork, 'grp', [(dev, dev ^ hop) for dev in range(16)])]
    all_to_all x1 -> x0, blocking collectives: 13.4 us -> none  [per_device(): lax.all_to_all(gradients[0], 'head', split_axis=0, concat_axis=2, tiled=T...]
    unnamed x83 -> x81, local copies, waits for them, and re-layouts: 32.9 us -> 30.2 us
  transfers between devices with their start and end apart: 11 -> 15, of which waited for: 6 -> 8; matrix products, arithmetic and copies ran while one was open for 52% -> 63% of each run, Pallas kernels for 0% -> 0%
where the time goes in v1:
time: 477 us; the launch traced here: 471 us
  other arithmetic  237 us (50%)
  starting transfers between devices  80.1 us (17%)
  matrix products  54.3 us (11%)
  waiting for transfers between devices  49 us (10%)
  local copies, waits for them, and re-layouts  48.5 us (10%)
    another operation x4, other arithmetic, decay_forward(): jax.scipy.linalg.solve_triangular(identity_block + coupling, target_outpu...  158 us
    unnamed x5, other arithmetic  57.8 us
    unnamed x81, local copies, waits for them, and re-layouts  30.2 us
    ppermute x4, waiting for transfers between devices, per_device(): lax.ppermute(grad_fork, 'grp', [(dev, dev ^ hop) for dev in range(16)])  21.1 us
    ppermute x4, starting transfers between devices, per_device(): lax.ppermute(grad_fork, 'grp', [(dev, dev ^ hop) for dev in range(16)])  15.9 us
    dot_general x3, matrix products, decay_forward(): jnp.einsum('led,ldf->lef', key_forward_rows, state_in, precision=upper_li...  10.9 us
    another operation x3, matrix products, decay_forward(): jax.scipy.linalg.solve_triangular(identity_block + coupling, target_outpu...  10.2 us
  transfers between devices with their start and end apart: 15, of which 8 were waited for; matrix products, arithmetic and copies ran while one was open for 63% of the time, Pallas kernels for 0%

profile of v1, /device:TPU:1, one launch (start us, length us, event | category | flops | bytes accessed | tf_op | source)
XLA Modules:
  0.0 470.7 jit_solution(14486415102797818273)
XLA Ops:
  2.0 7.6 %all-to-all-start.3 = ((bf16[1,128,16]{1,0,2:T(2,128)(2,1)}), bf16[1,128,16]{1,0,2:T(2,128)(2,1)S(1)}, u32[]{:S(2)}, u32[]{:S(2)}) async-start(bf16[1,128,16]{1,0,2:T(2,128)(2,1)} %copy.205), calls=%async_computation.3 | async-start | bytes 16384 | tf_op jit(solution)/shard_map/all_to_all | solution.py:130
  13.3 11.5 %reduce.13 = bf16[2048,128]{1,0:T(8,128)(2,1)S(1)} reduce(bf16[2048,1,128]{2,1,0:T(2,128)(2,1)S(1)} %bitcast.201, bf16[]{:T(256)} %broadcast.315), dimensions={1}, to_apply=%bitcast.156.reduce_sub_computation | reduce | bytes 1048578
  25.7 7.3 %all-to-all-start.5 = ((bf16[16,2,8192]{2,1,0:T(2,128)(2,1)}), bf16[16,2,8192]{2,1,0:T(2,128)(2,1)S(1)}, u32[]{:S(2)}, u32[]{:S(2)}) async-start(bf16[16,2,8192]{2,1,0:T(2,128)(2,1)} %reshape.506), calls=%async_computation.5 | async-start | bytes 1048576 | tf_op jit(solution)/shard_map/all_to_all | solution.py:125
  33.8 11.5 %reduce.10 = bf16[2048,128]{1,0:T(8,128)(2,1)S(1)} reduce(bf16[2048,1,128]{2,1,0:T(2,128)(2,1)S(1)} %bitcast.205, bf16[]{:T(256)} %broadcast.315), dimensions={1}, to_apply=%bitcast.158.reduce_sub_computation | reduce | bytes 1048578
  47.1 11.5 %reduce.11 = bf16[2048,128]{1,0:T(8,128)(2,1)S(1)} reduce(bf16[2048,1,128]{2,1,0:T(2,128)(2,1)S(1)} %bitcast.206, bf16[]{:T(256)} %broadcast.315), dimensions={1}, to_apply=%bitcast.162.reduce_sub_computation | reduce | bytes 1048578
  60.5 11.7 %reduce.12 = bf16[2048,128]{1,0:T(8,128)(2,1)S(1)} reduce(bf16[2048,1,128]{2,1,0:T(2,128)(2,1)S(1)} %bitcast.207, bf16[]{:T(256)} %broadcast.315), dimensions={1}, to_apply=%bitcast.160.reduce_sub_computation | reduce | bytes 1048578
  74.0 11.5 %reduce.14 = bf16[2048,128]{1,0:T(8,128)(2,1)S(1)} reduce(bf16[2048,1,128]{2,1,0:T(2,128)(2,1)S(1)} %bitcast.202, bf16[]{:T(256)} %broadcast.315), dimensions={1}, to_apply=%bitcast.164.reduce_sub_computation | reduce | bytes 1048578
  88.3 6.8 %all-to-all-start.1 = ((bf16[16,2,8192]{2,1,0:T(2,128)(2,1)}), bf16[16,2,8192]{2,1,0:T(2,128)(2,1)S(1)}, u32[]{:S(2)}, u32[]{:S(2)}) async-start(bf16[16,2,8192]{2,1,0:T(2,128)(2,1)} %reshape.508), calls=%async_computation.1 | async-start | bytes 1048576 | tf_op jit(solution)/shard_map/all_to_all | solution.py:126
  96.8 7.9 %all-to-all-done.1 = bf16[16,2,8192]{2,1,0:T(2,128)(2,1)S(1)} async-done(((bf16[16,2,8192]{2,1,0:T(2,128)(2,1)}), bf16[16,2,8192]{2,1,0:T(2,128)(2,1)S(1)}, u32[]{:S(2)}, u32[]{:S(2)}) %all-to-all-start.1) | async-done | bytes 524320 | tf_op jit(solution)/shard_map/all_to_all | solution.py:126
  104.7 4.6 all-to-all-start.2
  111.3 7.1 %all-to-all-done.2 = bf16[16,2,8192]{2,1,0:T(2,128)(2,1)} async-done(((bf16[16,2,8192]{2,1,0:T(2,128)(2,1)}), bf16[16,2,8192]{2,1,0:T(2,128)(2,1)}, u32[]{:S(2)}, u32[]{:S(2)}) %all-to-all-start.2) | async-done | bytes 524320 | tf_op jit(solution)/shard_map/all_to_all | solution.py:128
  118.4 4.2 all-to-all-start
  137.2 157.8 %custom-call.7 = f32[16,1,128,128]{2,3,1,0:T(8,128)} custom-call(f32[16,1,128,128]{3,2,1,0:T(8,128)S(1)} %add_bitcast_fusion), custom_call_target="InvertDiagBlocksLowerTriangular" | custom-call | tf_op jit(solution)/shard_map/jvp(vmap(jit(_solve_triangular)))/triangular_solve | solution.py:41
  295.0 6.6 %all-to-all-start.4 = ((bf16[16,2,8192]{2,1,0:T(2,128)(2,1)}), bf16[16,2,8192]{2,1,0:T(2,128)(2,1)}, u32[]{:S(2)}, u32[]{:S(2)}) async-start(bf16[16,2,8192]{2,1,0:T(2,128)(2,1)} %reshape.514), calls=%async_computation.4 | async-start | bytes 1048576 | tf_op jit(solution)/shard_map/all_to_all | solution.py:127
  356.6 4.6 collective-permute-start
  361.2 4.9 %multiply_reduce_fusion = (f32[16,128]{1,0:T(8,128)S(1)}, f32[16,128,128]{2,1,0:T(8,128)}) fusion(f32[16,128,128]{2,1,0:T(8,128)S(1)} %copy-done.17, f32[128,128]{1,0:T(8,128)S(1)} %get-tuple-element.57, f32[16,128,128]{1,2,0:T(8,128)} %fusion.62, f32[16,1,128,128]{2,3,1,0:T(8,128)} %custom-call.7, pred[128,128]{1,0:T(8,128)(4,1)S(1)} %get-tuple-element.55), kind=kOutput, calls=%fused_computation.48 | convolution fusion | flops 403961856 | bytes 4284416 | tf_op jit(solution)/shard_map/transpose(jvp(vmap(jit(_solve_triangular))))/triangular_solve/dot.0 | solution.py:41
  366.8 6.9 %all-to-all-start.10 = ((bf16[16,128,1]{1,2,0:T(2,128)(2,1)}), bf16[16,128,1]{1,2,0:T(2,128)(2,1)S(1)}, u32[]{:S(2)}, u32[]{:S(2)}) async-start(bf16[16,128,1]{1,2,0:T(2,128)(2,1)} %copy.235), calls=%async_computation.10 | async-start | bytes 16384 | tf_op jit(solution)/shard_map/all_to_all | solution.py:150
  390.6 6.8 %all-to-all-start.9 = ((bf16[16,128,128]{2,1,0:T(8,128)(2,1)}), bf16[16,128,128]{2,1,0:T(8,128)(2,1)}, u32[]{:S(2)}, u32[]{:S(2)}) async-start(bf16[16,128,128]{2,1,0:T(8,128)(2,1)} %copy.231), calls=%async_computation.9 | async-start | bytes 1048576 | tf_op jit(solution)/shard_map/all_to_all | solution.py:149
  417.3 4.2 all-to-all-done.6
  425.0 14.9 %collective-permute-done.2 = f32[8,1,128,128]{3,0,2,1:T(8,128)S(1)} collective-permute-done((f32[8,1,128,128]{3,0,2,1:T(8,128)S(1)}, f32[8,1,128,128]{3,0,2,1:T(8,128)S(1)}, u32[]{:S(2)}, u32[]{:S(2)}) %collective-permute-start.2) | collective-permute-done | bytes 524320 | tf_op jit(solution)/shard_map/ppermute | solution.py:154
  439.9 6.6 %collective-permute-start.3 = (f32[8,1,128,128]{3,0,2,1:T(8,128)S(1)}, f32[8,1,128,128]{3,0,2,1:T(8,128)S(1)}, u32[]{:S(2)}, u32[]{:S(2)}) collective-permute-start(f32[8,1,128,128]{3,0,2,1:T(8,128)S(1)} %add.94), channel_id=1, source_target_pairs={{0,128},{16,144},{32,160},{48,176},{64,192},{80,208},{96,224},{112... | collective-permute-start | bytes 1572872 | tf_op jit(solution)/shard_map/ppermute | solution.py:154
  446.5 6.3 %all-to-all-start.8 = ((bf16[16,128,128]{2,1,0:T(8,128)(2,1)}), bf16[16,128,128]{2,1,0:T(8,128)(2,1)S(1)}, u32[]{:S(2)}, u32[]{:S(2)}) async-start(bf16[16,128,128]{2,1,0:T(8,128)(2,1)} %get-tuple-element.43), calls=%async_computation.8 | async-start | bytes 1048576 | tf_op jit(solution)/shard_map/all_to_all | solution.py:148
  457.8 5.2 %all-to-all-done.8 = bf16[16,128,128]{2,1,0:T(8,128)(2,1)S(1)} async-done(((bf16[16,128,128]{2,1,0:T(8,128)(2,1)}), bf16[16,128,128]{2,1,0:T(8,128)(2,1)S(1)}, u32[]{:S(2)}, u32[]{:S(2)}) %all-to-all-start.8) | async-done | bytes 524320 | tf_op jit(solution)/shard_map/all_to_all | solution.py:148
  464.3 4.9 %collective-permute-done.3 = f32[8,1,128,128]{3,0,2,1:T(8,128)S(1)} collective-permute-done((f32[8,1,128,128]{3,0,2,1:T(8,128)S(1)}, f32[8,1,128,128]{3,0,2,1:T(8,128)S(1)}, u32[]{:S(2)}, u32[]{:S(2)}) %collective-permute-start.3) | collective-permute-done | bytes 524320 | tf_op jit(solution)/shard_map/ppermute | solution.py:154
  (152 shorter events, 136.0 us)
Async XLA Ops:
  0.6 85.9 %copy-start = (f32[8,1,128,128]{3,2,1,0:T(8,128)S(1)}, f32[8,1,128,128]{3,2,1,0:T(8,128)}, u32[]{:S(2)}) copy-start(f32[8,1,128,128]{3,2,1,0:T(8,128)} %param.17) | copy-start | bytes 1572868
  2.0 23.7 %all-to-all-start.3 = ((bf16[1,128,16]{1,0,2:T(2,128)(2,1)}), bf16[1,128,16]{1,0,2:T(2,128)(2,1)S(1)}, u32[]{:S(2)}, u32[]{:S(2)}) async-start(bf16[1,128,16]{1,0,2:T(2,128)(2,1)} %copy.205), calls=%async_computation.3 | async-start | bytes 16384 | tf_op jit(solution)/shard_map/all_to_all | solution.py:130
  25.7 7.3 %copy-start.23 = (bf16[1,128,2048]{2,1,0:T(8,128)(2,1)S(1)}, bf16[1,128,2048]{2,1,0:T(8,128)(2,1)}, u32[]{:S(2)}) copy-start(bf16[1,128,2048]{2,1,0:T(8,128)(2,1)} %param.12) | copy-start | bytes 1572868
  25.7 62.6 %all-to-all-start.5 = ((bf16[16,2,8192]{2,1,0:T(2,128)(2,1)}), bf16[16,2,8192]{2,1,0:T(2,128)(2,1)S(1)}, u32[]{:S(2)}, u32[]{:S(2)}) async-start(bf16[16,2,8192]{2,1,0:T(2,128)(2,1)} %reshape.506), calls=%async_computation.5 | async-start | bytes 1048576 | tf_op jit(solution)/shard_map/all_to_all | solution.py:125
  88.3 16.4 %all-to-all-start.1 = ((bf16[16,2,8192]{2,1,0:T(2,128)(2,1)}), bf16[16,2,8192]{2,1,0:T(2,128)(2,1)S(1)}, u32[]{:S(2)}, u32[]{:S(2)}) async-start(bf16[16,2,8192]{2,1,0:T(2,128)(2,1)} %reshape.508), calls=%async_computation.1 | async-start | bytes 1048576 | tf_op jit(solution)/shard_map/all_to_all | solution.py:126
  104.7 13.6 %all-to-all-start.2 = ((bf16[16,2,8192]{2,1,0:T(2,128)(2,1)}), bf16[16,2,8192]{2,1,0:T(2,128)(2,1)}, u32[]{:S(2)}, u32[]{:S(2)}) async-start(bf16[16,2,8192]{2,1,0:T(2,128)(2,1)} %reshape.512), calls=%async_computation.2 | async-start | bytes 1048576 | tf_op jit(solution)/shard_map/all_to_all | solution.py:128
  118.4 176.6 %all-to-all-start = ((bf16[16,2,8192]{2,1,0:T(2,128)(2,1)}), bf16[16,2,8192]{2,1,0:T(2,128)(2,1)}, u32[]{:S(2)}, u32[]{:S(2)}) async-start(bf16[16,2,8192]{2,1,0:T(2,128)(2,1)} %reshape.510), calls=%async_computation | async-start | bytes 1048576 | tf_op jit(solution)/shard_map/all_to_all | solution.py:129
  295.0 24.6 %all-to-all-start.4 = ((bf16[16,2,8192]{2,1,0:T(2,128)(2,1)}), bf16[16,2,8192]{2,1,0:T(2,128)(2,1)}, u32[]{:S(2)}, u32[]{:S(2)}) async-start(bf16[16,2,8192]{2,1,0:T(2,128)(2,1)} %reshape.514), calls=%async_computation.4 | async-start | bytes 1048576 | tf_op jit(solution)/shard_map/all_to_all | solution.py:127
  327.6 4.0 copy-start.18
  344.5 3.7 copy-start.5
  344.5 3.7 copy-start.22
  354.0 7.2 %copy-start.17 = (f32[16,128,128]{2,1,0:T(8,128)S(1)}, f32[16,128,128]{2,1,0:T(8,128)}, u32[]{:S(2)}) copy-start(f32[16,128,128]{2,1,0:T(8,128)} %copy-done.16) | copy-start | bytes 3145732
  356.6 40.9 %collective-permute-start = (f32[8,1,128,128]{3,0,2,1:T(8,128)}, f32[8,1,128,128]{3,0,2,1:T(8,128)}, u32[]{:S(2)}, u32[]{:S(2)}) collective-permute-start(f32[8,1,128,128]{3,0,2,1:T(8,128)} %convolution_bitcast_fusion.1), channel_id=1, source_target_pairs={{0,16},{16,0},{32,48},{48,32},{64,80},{80,64},{96,112},{112,96},{1... | collective-permute-start | bytes 1572872 | tf_op jit(solution)/shard_map/ppermute | solution.py:154
  366.8 23.9 %all-to-all-start.10 = ((bf16[16,128,1]{1,2,0:T(2,128)(2,1)}), bf16[16,128,1]{1,2,0:T(2,128)(2,1)S(1)}, u32[]{:S(2)}, u32[]{:S(2)}) async-start(bf16[16,128,1]{1,2,0:T(2,128)(2,1)} %copy.235), calls=%async_computation.10 | async-start | bytes 16384 | tf_op jit(solution)/shard_map/all_to_all | solution.py:150
  380.2 4.6 copy-start.13
  390.6 10.7 %copy-start.12 = (f32[16,128,128]{1,2,0:T(8,128)S(1)}, f32[16,128,128]{1,2,0:T(8,128)}, u32[]{:S(2)}) copy-start(f32[16,128,128]{1,2,0:T(8,128)} %copy-done.11) | copy-start | bytes 3145732
  390.6 17.4 %all-to-all-start.9 = ((bf16[16,128,128]{2,1,0:T(8,128)(2,1)}), bf16[16,128,128]{2,1,0:T(8,128)(2,1)}, u32[]{:S(2)}, u32[]{:S(2)}) async-start(bf16[16,128,128]{2,1,0:T(8,128)(2,1)} %copy.231), calls=%async_computation.9 | async-start | bytes 1048576 | tf_op jit(solution)/shard_map/all_to_all | solution.py:149
  397.5 3.8 copy-start.9
  399.6 13.3 %collective-permute-start.1 = (f32[8,1,128,128]{3,0,2,1:T(8,128)}, f32[8,1,128,128]{3,0,2,1:T(8,128)}, u32[]{:S(2)}, u32[]{:S(2)}) collective-permute-start(f32[8,1,128,128]{3,0,2,1:T(8,128)} %add.92), channel_id=1, source_target_pairs={{0,32},{16,48},{32,0},{48,16},{64,96},{80,112},{96,64},{112,80},{1... | collective-permute-start | bytes 1572872 | tf_op jit(solution)/shard_map/ppermute | solution.py:154
  408.1 13.4 %all-to-all-start.6 = ((bf16[16,128,128]{1,2,0:T(8,128)(2,1)}), bf16[16,128,128]{1,2,0:T(8,128)(2,1)S(1)}, u32[]{:S(2)}, u32[]{:S(2)}) async-start(bf16[16,128,128]{1,2,0:T(8,128)(2,1)} %get-tuple-element.45), calls=%async_computation.6 | async-start | bytes 1048576 | tf_op jit(solution)/shard_map/all_to_all | solution.py:146
  414.2 25.7 %collective-permute-start.2 = (f32[8,1,128,128]{3,0,2,1:T(8,128)S(1)}, f32[8,1,128,128]{3,0,2,1:T(8,128)S(1)}, u32[]{:S(2)}, u32[]{:S(2)}) collective-permute-start(f32[8,1,128,128]{3,0,2,1:T(8,128)S(1)} %add.93), channel_id=1, source_target_pairs={{0,64},{16,80},{32,96},{48,112},{64,0},{80,16},{96,32},{112,48},{1... | collective-permute-start | bytes 1572872 | tf_op jit(solution)/shard_map/ppermute | solution.py:154
  421.4 25.1 %all-to-all-start.7 = ((bf16[16,128,128]{1,2,0:T(8,128)(2,1)}), bf16[16,128,128]{1,2,0:T(8,128)(2,1)S(1)}, u32[]{:S(2)}, u32[]{:S(2)}) async-start(bf16[16,128,128]{1,2,0:T(8,128)(2,1)} %get-tuple-element.44), calls=%async_computation.7 | async-start | bytes 1048576 | tf_op jit(solution)/shard_map/all_to_all | solution.py:147
  439.9 29.3 %collective-permute-start.3 = (f32[8,1,128,128]{3,0,2,1:T(8,128)S(1)}, f32[8,1,128,128]{3,0,2,1:T(8,128)S(1)}, u32[]{:S(2)}, u32[]{:S(2)}) collective-permute-start(f32[8,1,128,128]{3,0,2,1:T(8,128)S(1)} %add.94), channel_id=1, source_target_pairs={{0,128},{16,144},{32,160},{48,176},{64,192},{80,208},{96,224},{112... | collective-permute-start | bytes 1572872 | tf_op jit(solution)/shard_map/ppermute | solution.py:154
  446.5 16.5 %all-to-all-start.8 = ((bf16[16,128,128]{2,1,0:T(8,128)(2,1)}), bf16[16,128,128]{2,1,0:T(8,128)(2,1)S(1)}, u32[]{:S(2)}, u32[]{:S(2)}) async-start(bf16[16,128,128]{2,1,0:T(8,128)(2,1)} %get-tuple-element.43), calls=%async_computation.8 | async-start | bytes 1048576 | tf_op jit(solution)/shard_map/all_to_all | solution.py:148
  (20 other events, 36.5 us)
